TPU v7x, 128 devices: a whole 4x4x4 slice. The times are simulated.
128 devices in a mesh: freq: 4 (over z_hi, core), pos: 32 (over x, y, z_lo).
Axes of the slice: x: 4, y: 4, z: 4 (z_hi: 2, z_lo: 2; z = z_hi * 2 + z_lo), core: 2. Of those that a mesh axis runs over, the one named last changes fastest.
Arguments:
- spectra: bfloat16 [16, 2, 256, 32768], P(None, None, 'freq', 'pos'), may hold values from -6 to 6
- green: bfloat16 [16, 32768, 2048], P('freq', 'pos'), may hold values from -0.0234375 to 0.0234375
- recorded: bfloat16 [256, 1024, 512], P('pos', 'freq'), may hold values from -6 to 6
- filter_taps: float32 [256, 11], P('pos'), may hold values from -3 to 3
Outputs:
- primaries: bfloat16 [256, 1024, 512], P('pos', 'freq')
All inputs are finite; a program needn't handle non-finite values.
Results may differ from a plain program's by a relative error of at most 0.001.
Values may be sent and summed in bfloat16 or wider, within the bound.
No kernel may reach another device: no remote copies, remote signals or barrier semaphores. Data moves between devices by JAX's collectives and lax.ppermute only.
A program may use at most 128 MiB of HBM per device.

v0:
```python
import jax
import jax.numpy as jnp
from jax import lax
from jax.sharding import Mesh
from jax.sharding import PartitionSpec as P

BAND_START = 32
FREQ = ("freq_0", "freq_1")
POS = ("pos_0", "pos_1", "pos_2")


def sum_by_axis(subtotal, axes):
    for axis in axes:
        subtotal = lax.psum_scatter(subtotal, axis, scatter_dimension=0, tiled=True)
    return subtotal


def cut_along(array, dim, devices):
    before, after = (array.shape[:dim], array.shape[dim + 1 :])
    return jnp.moveaxis(array.reshape(*before, devices, -1, *after), dim, 0)


def joined_along(parts, dim):
    shape = list(parts.shape[1:])
    shape[dim] *= parts.shape[0]
    return jnp.moveaxis(parts, 0, dim).reshape(shape)


def moved_by_axis(parts, axes, order):
    shape = [lax.axis_size(a) for a in axes]
    parts = parts.reshape(*shape, *parts.shape[1:])
    for k in order:
        parts = lax.all_to_all(parts, axes[k], split_axis=k, concat_axis=k, tiled=True)
    return parts.reshape(-1, *parts.shape[len(axes) :])


def core_and_chips(array, groups, order, split_dim, concat_dim):
    devices = lax.axis_size(groups[0]) * lax.axis_size(groups[1])
    parts = cut_along(array, split_dim, devices)
    return joined_along(moved_by_axis(parts, groups, order), concat_dim)


def phase_table(first_freq, freq_count, total_freqs, samples):
    bins = BAND_START + first_freq + jnp.arange(freq_count, dtype=jnp.int32)
    sample_index = jnp.arange(samples, dtype=jnp.int32)
    phase = bins[:, None] * sample_index[None, :] % samples
    angle = 2.0 * jnp.pi / samples * phase.astype(jnp.float32)
    scale = 1.0 / jnp.sqrt(jnp.float32(total_freqs))
    return jnp.stack([jnp.cos(angle), -jnp.sin(angle)], 1) * scale


def on_device(spectra, green, recorded, filter_taps):
    regrouped = lax.all_to_all(spectra, FREQ, split_axis=0, concat_axis=2, tiled=True)
    half_cols = green.shape[2] // 2
    product = jnp.einsum("fisk,fkr->sfir", regrouped, green, preferred_element_type=jnp.float32)
    real_part = product[:, :, 0, :half_cols] - product[:, :, 1, half_cols:]
    imag_part = product[:, :, 0, half_cols:] + product[:, :, 1, :half_cols]
    own_share = sum_by_axis(jnp.stack([real_part, imag_part], 2), POS)
    samples = recorded.shape[2]
    total_freqs = spectra.shape[0]
    spread = core_and_chips(own_share, ("freq_0", "freq_1"), (1, 0), 3, 1)
    table = phase_table(0, total_freqs, total_freqs, samples)
    traces = jnp.einsum("sfir,fit->srt", spread, table, precision=lax.Precision.HIGHEST)
    tap_count = filter_taps.shape[1]
    margin = (tap_count - 1) // 2
    padded = jnp.pad(traces, ((0, 0), (0, 0), (margin, margin)))
    result = recorded.astype(jnp.float32)
    for lag in range(tap_count):
        result = result - filter_taps[:, lag][:, None, None] * padded[:, :, lag : lag + samples]
    return result.astype(jnp.bfloat16)


def solution(mesh):
    torus = Mesh(
        mesh.devices.reshape(2, 2, 4, 4, 2), ("freq_0", "freq_1", "pos_0", "pos_1", "pos_2")
    )
    placed = (P(None, None, FREQ, POS), P(FREQ, POS, None), P(POS, FREQ, None), P(POS, None))
    return jax.shard_map(
        on_device, mesh=torus, in_specs=placed, out_specs=P(POS, FREQ, None), check_vma=False
    )
```

profile of v0, /device:TPU:0, one launch (start us, length us, event | category | flops | bytes accessed | tf_op | source)
XLA Modules:
  0.0 406.5 jit_solution(1218572337466034315)
XLA Ops:
  6.5 54.9 %all_to_all.28 = bf16[16,2,64,1024]{3,2,1,0:T(8,128)(2,1)S(1)} all-to-all(bf16[16,2,64,1024]{3,2,1,0:T(8,128)(2,1)} %param.4), channel_id=1, replica_groups=mesh['freq_0'=2,'freq_1'=2,'pos_0'=4,'pos_1'=4,'pos_2'=2] {'freq_0','fre..., dimensions={0} | all-to-all | bytes 8388608 | tf_op jit(solution)/shard_map/all_to_all | solution.py:53
  61.4 2.4 copy.19
  63.8 18.0 %fusion.2 = f32[256,4,2,2048]{0,3,2,1:T(8,128)} fusion(bf16[4,2,256,1024]{3,2,1,0:T(8,128)(2,1)} %bitcast.36, bf16[4,1024,2048]{2,1,0:T(8,128)(2,1)} %param.5), kind=kOutput, calls=%fused_computation.13 | convolution fusion | flops 8589934592 | bytes 37748736 | tf_op jit(solution)/shard_map/fisk,fkr->sfir/dot_general | solution.py:55
  81.8 9.2 %slice_subtract_fusion = (f32[256,4,1,1024]{0,3,2,1:T(8,128)S(1)}, f32[256,4,1,1024]{0,3,2,1:T(8,128)}) fusion(f32[256,4,2,2048]{0,3,2,1:T(8,128)} %fusion.2), kind=kLoop, calls=%fused_computation.36 | loop fusion | flops 2097152 | bytes 25165824 | tf_op jit(solution)/shard_map/sub | solution.py:56
  91.0 6.1 %pad_maximum_fusion = f32[256,4,2,1024]{0,3,2,1:T(8,128)} fusion(f32[256,4,1,1024]{0,3,2,1:T(8,128)} %get-tuple-element.17, f32[256,4,1,1024]{0,3,2,1:T(8,128)S(1)} %get-tuple-element.16), kind=kLoop, calls=%fused_computation.2 | loop fusion | flops 2097152 | bytes 16777216 | tf_op jit(solution)/shard_map/stack | solution.py:58
  97.1 10.5 %copy.21 = f32[256,4,2,1024]{3,1,2,0:T(4,128)} copy(f32[256,4,2,1024]{0,3,2,1:T(8,128)} %pad_maximum_fusion) | data formatting | bytes 16777216 | tf_op jit(solution)/shard_map/stack | solution.py:58
  107.7 0.5 copy-done.4
  108.3 0.6 dynamic-slice
  109.5 157.7 %all-reduce.8.cloned.1.call-done = f32[256,4,2,1024]{3,1,2,0:T(4,128)} async-done(((f32[256,4,2,1024]{3,1,2,0:T(4,128)}), f32[256,4,2,1024]{3,1,2,0:T(4,128)}) %all-reduce.8.cloned.1.call-update) | async-done | bytes 8388624
  267.2 3.2 constant_dynamic-slice_fusion.2
  270.5 0.6 dynamic-slice.2
  271.7 57.4 %all-reduce.10.cloned.1.call-done = f32[64,4,2,1024]{3,1,2,0:T(4,128)} async-done(((f32[64,4,2,1024]{3,1,2,0:T(4,128)}), f32[64,4,2,1024]{3,1,2,0:T(4,128)}) %all-reduce.10.cloned.1.call-update) | async-done | bytes 2097168
  329.2 1.9 constant_dynamic-slice_fusion.1
  331.1 0.7 dynamic-slice.4
  332.5 34.4 %all-reduce.12.cloned.1.call-done = f32[16,4,2,1024]{3,1,2,0:T(4,128)} async-done(((f32[16,4,2,1024]{3,1,2,0:T(4,128)}), f32[16,4,2,1024]{3,1,2,0:T(4,128)}) %all-reduce.12.cloned.1.call-update) | async-done | bytes 524304
  366.8 1.0 constant_dynamic-slice_fusion
  368.2 4.1 %all_to_all.29 = f32[2,2,8,4,2,256]{5,2,4,3,0,1:T(8,128)S(1)} all-to-all(f32[2,2,8,4,2,256]{5,2,4,3,0,1:T(8,128)S(1)} %copy.24), channel_id=1, replica_groups=mesh['freq_0'=2,'freq_1'=2,'pos_0'=4,'pos_1'=4,'pos_2'=2] {'freq_1'}, dimensions={1} | all-to-all | bytes 524288 | tf_op jit(solution)/shard_map/all_to_all | solution.py:33
  372.3 0.7 copy.25
  373.0 4.1 %all-to-all-start.2 = ((f32[2,2,8,4,2,256]{5,2,4,3,1,0:T(8,128)}), f32[2,2,8,4,2,256]{5,2,4,3,1,0:T(8,128)S(1)}, u32[]{:S(2)}, u32[]{:S(2)}) async-start(f32[2,2,8,4,2,256]{5,2,4,3,1,0:T(8,128)} %copy.25), calls=%async_computation.2 | async-start | bytes 524288 | tf_op jit(solution)/shard_map/all_to_all | solution.py:33
  377.1 0.2 fusion.38
  377.3 0.3 slice_reduce_fusion.10
  377.7 6.4 %all-to-all-done.2 = f32[2,2,8,4,2,256]{5,2,4,3,1,0:T(8,128)S(1)} async-done(((f32[2,2,8,4,2,256]{5,2,4,3,1,0:T(8,128)}), f32[2,2,8,4,2,256]{5,2,4,3,1,0:T(8,128)S(1)}, u32[]{:S(2)}, u32[]{:S(2)}) %all-to-all-start.2) | async-done | bytes 262176 | tf_op jit(solution)/shard_map/all_to_all | solution.py:33
  384.4 3.5 convolution_bitcast_fusion
  387.9 12.1 %fusion.26 = bf16[8,256,512]{2,1,0:T(8,128)(2,1)} fusion(f32[8,256,512]{2,1,0:T(8,128)S(1)} %convolution_bitcast_fusion, bf16[8,256,512]{2,1,0:T(8,128)(2,1)S(1)} %copy-done, f32[8]{0:T(128)S(1)} %get-tuple-element.14, f32[8]{0:T(128)S(1)} %get-tuple-element.15, f32[8]{0:T(128)S(1)} %get-tuple-element.6, f32[8]{0:T(128)S(1)} %get-tuple-element.7, ...), kind=kLoop, calls=%fused_computation.37 | loop fusion | flops 25165824 | bytes 8388960 | tf_op jit(solution)/shard_map/convert_element_type | solution.py:70
  (21 shorter events, 0.8 us)
Async XLA Ops:
  6.5 260.7 %all-reduce.8.cloned.1.call-start = ((), (), s32[]{:S(2)}) async-start(), calls=%async_computation.3 | async-start | bytes 16777216
  107.6 0.7 copy-start.4
  107.6 162.9 %copy-start.3 = (u32[128]{0:T(128)S(1)}, u32[128]{0:T(128)}, u32[]{:S(2)}) copy-start(u32[128]{0:T(128)} %constant.34) | copy-start | bytes 1540
  107.6 223.4 %copy-start.2 = (u32[128]{0:T(128)S(1)}, u32[128]{0:T(128)}, u32[]{:S(2)}) copy-start(u32[128]{0:T(128)} %constant.38) | copy-start | bytes 1540
  107.7 221.5 %all-reduce.10.cloned.1.call-start = ((), (), s32[]{:S(2)}) async-start(), calls=%async_computation.4 | async-start | bytes 4194304
  270.4 106.9 %copy-start.1 = (f32[8,11]{1,0:T(8,128)S(1)}, f32[8,11]{1,0:T(8,128)}, u32[]{:S(2)}) copy-start(f32[8,11]{1,0:T(8,128)} %param.7) | copy-start | bytes 1060
  270.5 96.4 %all-reduce.12.cloned.1.call-start = ((), (), s32[]{:S(2)}) async-start(), calls=%async_computation.5 | async-start | bytes 1048576
  368.0 19.9 %copy-start = (bf16[8,256,512]{2,1,0:T(8,128)(2,1)S(1)}, bf16[8,256,512]{2,1,0:T(8,128)(2,1)}, u32[]{:S(2)}) copy-start(bf16[8,256,512]{2,1,0:T(8,128)(2,1)} %param.6) | copy-start | bytes 6291460
  373.0 11.1 %all-to-all-start.2 = ((f32[2,2,8,4,2,256]{5,2,4,3,1,0:T(8,128)}), f32[2,2,8,4,2,256]{5,2,4,3,1,0:T(8,128)S(1)}, u32[]{:S(2)}, u32[]{:S(2)}) async-start(f32[2,2,8,4,2,256]{5,2,4,3,1,0:T(8,128)} %copy.25), calls=%async_computation.2 | async-start | bytes 524288 | tf_op jit(solution)/shard_map/all_to_all | solution.py:33
Sparse Core Ops, SparseCore 0:
  107.8 159.4 all-reduce.7
  270.6 58.5 all-reduce.9
  331.6 35.1 all-reduce.11
where the time goes:
time: 407 us; the launch traced here: 406 us
  waiting for transfers between devices  256 us (63%)
  blocking collectives  59 us (14%)
  other arithmetic  27.6 us (7%)
  local copies, waits for them, and re-layouts  23 us (6%)
  matrix products  21.5 us (5%)
  between operations  15.2 us (4%)
  starting transfers between devices  4.21 us (1%)
    unnamed x6, waiting for transfers between devices  250 us
    all_to_all x1, blocking collectives, on_device(): lax.all_to_all(spectra, FREQ, split_axis=0, concat_axis=2, tiled=True)  54.9 us
    dot_general x1, matrix products, on_device(): jnp.einsum('fisk,fkr->sfir', regrouped, green, preferred_element_type=jnp...  18 us
    convert_element_type x1, other arithmetic, on_device(): return result.astype(jnp.bfloat16)  12.1 us
    another operation x1, local copies, waits for them, and re-layouts, on_device(): own_share = sum_by_axis(jnp.stack([real_part, imag_part], 2), POS)  10.5 us
    sub x1, other arithmetic, on_device(): real_part = product[:, :, 0, :half_cols] - product[:, :, 1, half_cols:]  9.15 us
    unnamed x16, local copies, waits for them, and re-layouts  8.49 us
  transfers between devices with their start and end apart: 4, of which 4 were waited for; matrix products, arithmetic and copies ran while one was open for 1% of the time, Pallas kernels for 0%

commit v1 on v0

--- a/solution.py
+++ b/solution.py
@@ -50,7 +50,9 @@
 
 
 def on_device(spectra, green, recorded, filter_taps):
-    regrouped = lax.all_to_all(spectra, FREQ, split_axis=0, concat_axis=2, tiled=True)
+    regrouped = jnp.concatenate(
+        lax.all_to_all(jnp.stack(jnp.split(spectra, lax.axis_size(FREQ), 0), 0), FREQ, 0, 0), 2
+    )
     half_cols = green.shape[2] // 2
     product = jnp.einsum("fisk,fkr->sfir", regrouped, green, preferred_element_type=jnp.float32)
     real_part = product[:, :, 0, :half_cols] - product[:, :, 1, half_cols:]

time: 407 us -> 268 us (0.66)
  waiting for transfers between devices: 256 us -> 138 us
  local copies, waits for them, and re-layouts: 23 us -> 5.37 us
    unnamed x6 -> x3, waiting for transfers between devices: 250 us -> 0.05 us
    reduce_scatter x0 -> x3, waiting for transfers between devices: none -> 131 us  [sum_by_axis(): subtotal = lax.psum_scatter(subtotal, axis, scatter_dimension=0, tiled=True)]
    unnamed x16 -> x4, local copies, waits for them, and re-layouts: 8.49 us -> 0.01 us
    another operation x1, local copies, waits for them, and re-layouts: 10.5 us -> 2.87 us  [on_device(): jnp.stack(jnp.split(spectra, lax.axis_size(FREQ), 0), 0)]
  transfers between devices with their start and end apart: 4 -> 4, of which waited for: 4 -> 4; matrix products, arithmetic and copies ran while one was open for 1% -> 0% of each run, Pallas kernels for 0% -> 0%
where the time goes in v1:
time: 268 us
  waiting for transfers between devices  138 us (51%)
  blocking collectives  58.6 us (22%)
  other arithmetic  29.8 us (11%)
  matrix products  19.1 us (7%)
  between operations  13.2 us (5%)
  local copies, waits for them, and re-layouts  5.37 us (2%)
  starting transfers between devices  4.21 us (2%)
    reduce_scatter x3, waiting for transfers between devices, sum_by_axis(): subtotal = lax.psum_scatter(subtotal, axis, scatter_dimension=0, tiled=True)  131 us
    all_to_all x1, blocking collectives, on_device(): lax.all_to_all(jnp.stack(jnp.split(spectra, lax.axis_size(FREQ), 0), 0),...  54.7 us
    dot_general x1, matrix products, on_device(): jnp.einsum('fisk,fkr->sfir', regrouped, green, preferred_element_type=jnp...  15.6 us
    convert_element_type x1, other arithmetic, on_device(): return result.astype(jnp.bfloat16)  12.1 us
    sub x1, other arithmetic, on_device(): real_part = product[:, :, 0, :half_cols] - product[:, :, 1, half_cols:]  10.3 us
    another operation x1, other arithmetic, on_device(): own_share = sum_by_axis(jnp.stack([real_part, imag_part], 2), POS)  6.65 us
    all_to_all x1, waiting for transfers between devices, moved_by_axis(): lax.all_to_all(parts, axes[k], split_axis=k, concat_axis=k, tiled=True)  6.42 us
  transfers between devices with their start and end apart: 4, of which 4 were waited for; matrix products, arithmetic and copies ran while one was open for 0% of the time, Pallas kernels for 0%

profile of v1, /device:TPU:0, one launch (start us, length us, event | category | flops | bytes accessed | tf_op | source)
XLA Modules:
  0.0 267.9 jit_solution(11939591765964721156)
XLA Ops:
  6.5 2.9 %slice_bitcast_fusion.3 = (bf16[1,4,2,64,1024]{4,3,2,1,0:T(8,128)(2,1)S(1)}, bf16[1,4,2,64,1024]{4,3,2,1,0:T(8,128)(2,1)S(1)}, bf16[1,4,2,64,1024]{4,3,2,1,0:T(8,128)(2,1)S(1)}, bf16[1,4,2,64,1024]{4,3,2,1,0:T(8,128)(2,1)S(1)}) fusion(bf16[16,2,64,1024]{3,2,1,0:T(8,128)(2,1)} %param.4), kind=kLoop, calls=%fused_computation.43 | loop fusion | bytes 8388608 | tf_op jit(solution)/shard_map/stack | solution.py:54
  9.4 0.6 pad_maximum_fusion.1
  10.0 54.7 %all_to_all.15 = bf16[4,4,2,64,1024]{4,3,2,1,0:T(8,128)(2,1)S(1)} all-to-all(bf16[4,4,2,64,1024]{4,3,2,1,0:T(8,128)(2,1)S(1)} %pad_maximum_fusion.1), channel_id=1, replica_groups=mesh['freq_0'=2,'freq_1'=2,'pos_0'=4,'pos_1'=4,'pos_2'=2] {'freq_0','fre..., dimensions={0} | all-to-all | bytes 8388608 | tf_op jit(solution)/shard_map/all_to_all | solution.py:54
  64.7 0.4 copy.9
  65.1 15.6 %fusion.2 = f32[256,4,2,2048]{3,0,2,1:T(8,128)} fusion(bf16[4,2,256,1024]{3,2,1,0:T(8,128)(2,1)S(1)} %bitcast.37, bf16[4,1024,2048]{2,1,0:T(8,128)(2,1)} %param.5), kind=kOutput, calls=%fused_computation.13 | convolution fusion | flops 8589934592 | bytes 37748736 | tf_op jit(solution)/shard_map/fisk,fkr->sfir/dot_general | solution.py:57
  80.8 10.3 %slice_subtract_fusion = (f32[256,4,1,1024]{3,0,2,1:T(8,128)S(1)}, f32[256,4,1,1024]{3,0,2,1:T(8,128)}) fusion(f32[256,4,2,2048]{3,0,2,1:T(8,128)} %fusion.2), kind=kLoop, calls=%fused_computation.36 | loop fusion | flops 2097152 | bytes 25165824 | tf_op jit(solution)/shard_map/sub | solution.py:58
  91.1 6.7 %pad_maximum_fusion = f32[256,4,2,1024]{3,0,2,1:T(8,128)} fusion(f32[256,4,1,1024]{3,0,2,1:T(8,128)} %get-tuple-element.17, f32[256,4,1,1024]{3,0,2,1:T(8,128)S(1)} %get-tuple-element.16), kind=kLoop, calls=%fused_computation.2 | loop fusion | flops 2097152 | bytes 16777216 | tf_op jit(solution)/shard_map/stack | solution.py:60
  97.7 0.0 reduce-scatter.4.cloned.1.call-update
  97.8 0.0 reduce-scatter.6.cloned.1.call-start
  97.8 79.9 %reduce-scatter.4.cloned.1.call-done = f32[64,4,2,1024]{3,0,2,1:T(8,128)} async-done(((f32[256,4,2,1024]{3,0,2,1:T(8,128)}), f32[64,4,2,1024]{3,0,2,1:T(8,128)}) %reduce-scatter.4.cloned.1.call-update) | async-done | bytes 2097168 | tf_op jit(solution)/shard_map/reduce_scatter | solution.py:14
  177.8 0.0 reduce-scatter.6.cloned.1.call-update
  177.8 0.0 reduce-scatter.8.cloned.1.call-start
  177.8 31.8 %reduce-scatter.6.cloned.1.call-done = f32[16,4,2,1024]{3,0,2,1:T(8,128)} async-done(((f32[64,4,2,1024]{3,0,2,1:T(8,128)}), f32[16,4,2,1024]{3,0,2,1:T(8,128)}) %reduce-scatter.6.cloned.1.call-update) | async-done | bytes 524304 | tf_op jit(solution)/shard_map/reduce_scatter | solution.py:14
  209.7 0.0 reduce-scatter.8.cloned.1.call-update
  209.7 19.3 %reduce-scatter.8.cloned.1.call-done = f32[8,4,2,1024]{3,0,2,1:T(8,128)} async-done(((f32[16,4,2,1024]{3,0,2,1:T(8,128)}), f32[8,4,2,1024]{3,0,2,1:T(8,128)}) %reduce-scatter.8.cloned.1.call-update) | async-done | bytes 262160 | tf_op jit(solution)/shard_map/reduce_scatter | solution.py:14
  229.0 1.0 copy.11
  230.0 3.9 %all_to_all.16 = f32[2,2,8,4,2,256]{5,2,0,4,3,1:T(8,128)S(1)} all-to-all(f32[2,2,8,4,2,256]{5,2,0,4,3,1:T(8,128)S(1)} %copy.11), channel_id=1, replica_groups=mesh['freq_0'=2,'freq_1'=2,'pos_0'=4,'pos_1'=4,'pos_2'=2] {'freq_1'}, dimensions={1} | all-to-all | bytes 524288 | tf_op jit(solution)/shard_map/all_to_all | solution.py:33
  233.9 0.7 copy.12
  234.6 4.1 %all-to-all-start.2 = ((f32[2,2,8,4,2,256]{5,2,1,4,3,0:T(8,128)}), f32[2,2,8,4,2,256]{5,2,1,4,3,0:T(8,128)S(1)}, u32[]{:S(2)}, u32[]{:S(2)}) async-start(f32[2,2,8,4,2,256]{5,2,1,4,3,0:T(8,128)} %copy.12), calls=%async_computation.5 | async-start | bytes 524288 | tf_op jit(solution)/shard_map/all_to_all | solution.py:33
  238.8 0.2 fusion.39
  239.0 0.3 slice_reduce_fusion.10
  239.3 6.4 %all-to-all-done.2 = f32[2,2,8,4,2,256]{5,2,1,4,3,0:T(8,128)S(1)} async-done(((f32[2,2,8,4,2,256]{5,2,1,4,3,0:T(8,128)}), f32[2,2,8,4,2,256]{5,2,1,4,3,0:T(8,128)S(1)}, u32[]{:S(2)}, u32[]{:S(2)}) %all-to-all-start.2) | async-done | bytes 262176 | tf_op jit(solution)/shard_map/all_to_all | solution.py:33
  245.8 3.5 %convolution_bitcast_fusion = f32[8,256,512]{2,1,0:T(8,128)S(1)} fusion(f32[8,16,2,256]{3,0,2,1:T(8,128)S(1)} %bitcast.38, f32[16,1,512]{2,0,1:T(8,128)S(1)} %get-tuple-element.23, f32[16,1,512]{2,0,1:T(8,128)S(1)} %get-tuple-element.22), kind=kOutput, calls=%fused_computation.39 | convolution fusion | flops 402685952 | bytes 4521984 | tf_op jit(solution)/shard_map/sfir,fit->srt/dot_general | solution.py:65
  249.3 12.1 %fusion.26 = bf16[8,256,512]{2,1,0:T(8,128)(2,1)} fusion(f32[8,256,512]{2,1,0:T(8,128)S(1)} %convolution_bitcast_fusion, bf16[8,256,512]{2,1,0:T(8,128)(2,1)S(1)} %copy-done, f32[8]{0:T(128)S(1)} %get-tuple-element.14, f32[8]{0:T(128)S(1)} %get-tuple-element.15, f32[8]{0:T(128)S(1)} %get-tuple-element.6, f32[8]{0:T(128)S(1)} %get-tuple-element.7, ...), kind=kLoop, calls=%fused_computation.38 | loop fusion | flops 25165824 | bytes 8388960 | tf_op jit(solution)/shard_map/convert_element_type | solution.py:72
  (7 shorter events, 0.0 us)
Async XLA Ops:
  6.5 171.2 %reduce-scatter.4.cloned.1.call-start = ((), (), s32[]{:S(2)}) async-start(), calls=%async_computation.6 | async-start | bytes 10485760 | tf_op jit(solution)/shard_map/reduce_scatter | solution.py:14
  97.7 141.2 %copy-start.1 = (f32[8,11]{1,0:T(8,128)S(1)}, f32[8,11]{1,0:T(8,128)}, u32[]{:S(2)}) copy-start(f32[8,11]{1,0:T(8,128)} %param.7) | copy-start | bytes 1060
  97.8 111.9 %reduce-scatter.6.cloned.1.call-start = ((), (), s32[]{:S(2)}) async-start(), calls=%async_computation.7 | async-start | bytes 2621440 | tf_op jit(solution)/shard_map/reduce_scatter | solution.py:14
  177.8 71.5 %copy-start = (bf16[8,256,512]{2,1,0:T(8,128)(2,1)S(1)}, bf16[8,256,512]{2,1,0:T(8,128)(2,1)}, u32[]{:S(2)}) copy-start(bf16[8,256,512]{2,1,0:T(8,128)(2,1)} %param.6) | copy-start | bytes 6291460
  177.8 51.2 %reduce-scatter.8.cloned.1.call-start = ((), (), s32[]{:S(2)}) async-start(), calls=%async_computation.8 | async-start | bytes 786432 | tf_op jit(solution)/shard_map/reduce_scatter | solution.py:14
  234.6 11.1 %all-to-all-start.2 = ((f32[2,2,8,4,2,256]{5,2,1,4,3,0:T(8,128)}), f32[2,2,8,4,2,256]{5,2,1,4,3,0:T(8,128)S(1)}, u32[]{:S(2)}, u32[]{:S(2)}) async-start(f32[2,2,8,4,2,256]{5,2,1,4,3,0:T(8,128)} %copy.12), calls=%async_computation.5 | async-start | bytes 524288 | tf_op jit(solution)/shard_map/all_to_all | solution.py:33
Sparse Core Ops, SparseCore 0:
  97.9 79.8 reduce-scatter.3
  180.2 29.4 reduce-scatter.5
  212.0 16.9 reduce-scatter.7
